TPU v7x, 256 devices: a whole 4x4x8 slice. The times are simulated.
256 devices in a mesh: st: 128 (over z, x_lo, y, core), row: 2 (over x_hi).
Axes of the slice: x: 4 (x_hi: 2, x_lo: 2; x = x_hi * 2 + x_lo), y: 4, z: 8, core: 2. Of those that a mesh axis runs over, the one named last changes fastest.
Arguments:
- forcing: bfloat16 [2, 128, 1024, 256], P(None, 'st', 'row'), may hold values from -6 to 6
- inverse_first: bfloat16 [2, 128, 1024, 1024], P(None, 'st', 'row'), may hold values from -0.1875 to 0.1875
- lower_first: bfloat16 [2, 128, 1024, 1024], P(None, 'st', 'row'), may hold values from -0.1875 to 0.1875
- upper_first: bfloat16 [2, 128, 1024, 1024], P(None, 'st', 'row'), may hold values from -0.1875 to 0.1875
- inverse_second: bfloat16 [2, 128, 1024, 1024], P(None, 'st', 'row'), may hold values from -0.1875 to 0.1875
- lower_second: bfloat16 [2, 128, 1024, 1024], P(None, 'st', 'row'), may hold values from -0.1875 to 0.1875
- upper_second: bfloat16 [2, 128, 1024, 1024], P(None, 'st', 'row'), may hold values from -0.1875 to 0.1875
Outputs:
- reduced_forcing: bfloat16 [2, 128, 1024, 256], P(None, 'st', 'row')
All inputs are finite; a program needn't handle non-finite values.
Results may differ from a plain program's by a relative error of at most 0.0059.
Values may be sent and summed in bfloat16 or wider, within the bound.
No kernel may reach another device: no remote copies, remote signals or barrier semaphores. Data moves between devices by JAX's collectives and lax.ppermute only.
A program may use at most 64 MiB of HBM per device.

v0:
```python
import jax
import jax.numpy as jnp
from jax import lax
from jax.sharding import PartitionSpec as P


def from_behind(value, axis, steps):
    count = lax.axis_size(axis)
    pairs = [(source, (source + steps) % count) for source in range(count)]
    return lax.ppermute(value, axis, pairs)


def shifted_earlier(received, stride):
    position = lax.axis_index("st")
    earlier = jnp.concatenate([jnp.zeros_like(received[:1]), received[:-1]], axis=0)
    return jnp.where(position < stride, earlier, received)


def shifted_later(received, stride):
    position = lax.axis_index("st")
    later_rows = jnp.concatenate([received[1:], jnp.zeros_like(received[:1])], axis=0)
    return jnp.where(position >= lax.axis_size("st") - stride, later_rows, received)


def product(blocks, vectors):
    return jnp.einsum("jrk,jkc->jrc", blocks, vectors, preferred_element_type=jnp.float32)


def reduce_level(forcing_now, inverse, lower, upper, stride):
    scaled = product(inverse, lax.all_gather(forcing_now, "row", axis=1, tiled=True)).astype(
        jnp.bfloat16
    )
    gathered = lax.all_gather(scaled, "row", axis=1, tiled=True)
    from_below = shifted_earlier(from_behind(gathered, "st", stride), stride)
    from_above = shifted_later(from_behind(gathered, "st", -stride), stride)
    coupled = product(lower, from_below) + product(upper, from_above)
    return (forcing_now.astype(jnp.float32) - coupled).astype(jnp.bfloat16)


def on_device(
    forcing, inverse_first, lower_first, upper_first, inverse_second, lower_second, upper_second
):

    def squeeze(array):
        return array.reshape((array.shape[0],) + array.shape[2:])

    forcing_first = reduce_level(
        squeeze(forcing), squeeze(inverse_first), squeeze(lower_first), squeeze(upper_first), 1
    )
    reduced = reduce_level(
        forcing_first, squeeze(inverse_second), squeeze(lower_second), squeeze(upper_second), 2
    )
    return reduced.reshape(forcing.shape)


def solution(mesh):
    return jax.shard_map(
        on_device,
        mesh=mesh,
        in_specs=(
            P(None, "st", "row", None),
            P(None, "st", "row", None),
            P(None, "st", "row", None),
            P(None, "st", "row", None),
            P(None, "st", "row", None),
            P(None, "st", "row", None),
            P(None, "st", "row", None),
        ),
        out_specs=P(None, "st", "row", None),
        check_vma=False,
    )
```

profile of v0, /device:TPU:1, one launch (start us, length us, event | category | flops | bytes accessed | tf_op | source)
XLA Modules:
  0.0 201.1 jit_solution(2558496426390451680)
XLA Ops:
  6.5 0.7 all-gather.12.cloned.1.call-update
  7.3 33.3 %all-gather.12.cloned.1.call-done = bf16[2,1,1024,256]{3,2,0,1:T(8,128)(2,1)} async-done(((bf16[2,1,512,256]{3,2,0,1:T(8,128)(2,1)}), bf16[2,1,1024,256]{3,2,0,1:T(8,128)(2,1)}) %all-gather.12.cloned.1.call-update) | async-done | bytes 1048592 | tf_op jit(solution)/shard_map/all_gather | solution.py:30
  40.7 2.7 %fusion.27 = bf16[2,512,256]{2,1,0:T(8,128)(2,1)} fusion(bf16[2,1,512,1024]{3,2,1,0:T(8,128)(2,1)S(1)} %copy-done, bf16[2,1,1024,256]{3,2,0,1:T(8,128)(2,1)} %all-gather.12.cloned.1.call-done), kind=kOutput, calls=%fused_computation.17 | convolution fusion | flops 537133056 | bytes 3670016 | tf_op jit(solution)/shard_map/jrk,jkc->jrc/dot_general | solution.py:26
  43.5 27.4 %all-gather.6.cloned.1.call-done = bf16[2,1024,256]{2,1,0:T(8,128)(2,1)} async-done(((bf16[2,512,256]{2,1,0:T(8,128)(2,1)}), bf16[2,1024,256]{2,1,0:T(8,128)(2,1)}) %all-gather.6.cloned.1.call-update) | async-done | bytes 1048592 | tf_op jit(solution)/shard_map/all_gather | solution.py:33
  70.9 0.8 collective-permute-start.1
  71.7 1.1 collective-permute-start
  72.8 0.2 copy.8
  73.1 12.9 %collective-permute-done.1 = bf16[2,1024,256]{2,1,0:T(8,128)(2,1)} collective-permute-done((bf16[2,1024,256]{2,1,0:T(8,128)(2,1)}, bf16[2,1024,256]{2,1,0:T(8,128)(2,1)}, u32[]{:S(2)}, u32[]{:S(2)}) %collective-permute-start.1) | collective-permute-done | bytes 1048608 | tf_op jit(solution)/shard_map/ppermute | solution.py:10
  85.9 1.1 slice.17
  87.0 1.1 slice.16
  88.1 2.9 %fusion.6 = f32[2,256,512]{2,1,0:T(8,128)S(1)} fusion(bf16[2,1,512,1024]{3,2,1,0:T(8,128)(2,1)} %param.10, bf16[2,1024,256]{2,1,0:T(8,128)(2,1)} %collective-permute-done.1, bf16[1,1024,256]{2,1,0:T(8,128)(2,1)S(1)} %slice.17, pred[]{:T(512)S(6)} %ge.6), kind=kOutput, calls=%fused_computation.6 | convolution fusion | flops 537395200 | bytes 4718593 | tf_op jit(solution)/shard_map/jrk,jkc->jrc/dot_general | solution.py:26
  91.1 3.1 %fusion.33 = bf16[2,512,256]{1,2,0:T(8,128)(2,1)} fusion(f32[2,256,512]{2,1,0:T(8,128)S(1)} %fusion.6, bf16[2,1,512,1024]{3,2,1,0:T(8,128)(2,1)S(1)} %copy-done.4, bf16[2,1024,256]{2,1,0:T(8,128)(2,1)} %collective-permute-done, bf16[1,1024,256]{2,1,0:T(8,128)(2,1)S(1)} %slice.16, pred[]{:T(512)S(6)} %lt.6, bf16[2,1,512,256]{2,3,0,1:T(8,128)(2,1)S(1)} %copy.8), kind=kOutput, calls=%fused_computation.19 | convolution fusion | flops 538443776 | bytes 5767169 | tf_op jit(solution)/shard_map/jrk,jkc->jrc/dot_general | solution.py:26
  94.2 0.0 all-gather.10.cloned.1.call-start
  94.3 30.5 %all-gather.8.cloned.1.call-done = bf16[2,1024,256]{1,2,0:T(8,128)(2,1)} async-done(((bf16[2,512,256]{1,2,0:T(8,128)(2,1)}), bf16[2,1024,256]{1,2,0:T(8,128)(2,1)}) %all-gather.8.cloned.1.call-update) | async-done | bytes 1048592 | tf_op jit(solution)/shard_map/all_gather | solution.py:30
  124.7 3.5 %fusion.36 = bf16[2,512,256]{1,2,0:T(8,128)(2,1)} fusion(bf16[2,1024,256]{1,2,0:T(8,128)(2,1)} %all-gather.8.cloned.1.call-done, bf16[2,1,512,1024]{3,2,1,0:T(8,128)(2,1)} %param.11), kind=kOutput, calls=%fused_computation.20 | convolution fusion | flops 537133056 | bytes 3670016 | tf_op jit(solution)/shard_map/jrk,jkc->jrc/dot_general | solution.py:26
  128.2 27.5 %all-gather.10.cloned.1.call-done = bf16[2,1024,256]{1,2,0:T(8,128)(2,1)} async-done(((bf16[2,512,256]{1,2,0:T(8,128)(2,1)}), bf16[2,1024,256]{1,2,0:T(8,128)(2,1)}) %all-gather.10.cloned.1.call-update) | async-done | bytes 1048592 | tf_op jit(solution)/shard_map/all_gather | solution.py:33
  155.7 5.2 %collective-permute-start.3 = (bf16[2,1024,256]{1,2,0:T(8,128)(2,1)}, bf16[2,1024,256]{1,2,0:T(8,128)(2,1)}, u32[]{:S(2)}, u32[]{:S(2)}) collective-permute-start(bf16[2,1024,256]{1,2,0:T(8,128)(2,1)} %all-gather.10.cloned.1.call-done), channel_id=1, source_target_pairs={{0,252},{2,254},{4,0},{6,2},{8,4},{10,6},{12,8},{14,10},{16,12},{1... | collective-permute-start | bytes 3145736 | tf_op jit(solution)/shard_map/ppermute | solution.py:10
  161.0 22.0 %collective-permute-done.3 = bf16[2,1024,256]{1,2,0:T(8,128)(2,1)} collective-permute-done((bf16[2,1024,256]{1,2,0:T(8,128)(2,1)}, bf16[2,1024,256]{1,2,0:T(8,128)(2,1)}, u32[]{:S(2)}, u32[]{:S(2)}) %collective-permute-start.3) | collective-permute-done | bytes 1048608 | tf_op jit(solution)/shard_map/ppermute | solution.py:10
  182.9 1.1 slice.19
  184.0 5.0 %collective-permute-done.2 = bf16[2,1024,256]{1,2,0:T(8,128)(2,1)S(1)} collective-permute-done((bf16[2,1024,256]{1,2,0:T(8,128)(2,1)}, bf16[2,1024,256]{1,2,0:T(8,128)(2,1)S(1)}, u32[]{:S(2)}, u32[]{:S(2)}) %collective-permute-start.2) | collective-permute-done | bytes 1048608 | tf_op jit(solution)/shard_map/ppermute | solution.py:10
  189.0 0.9 copy-done.3
  190.0 2.8 %fusion = f32[2,256,512]{2,1,0:T(8,128)S(1)} fusion(bf16[2,1,512,1024]{3,2,1,0:T(8,128)(2,1)} %param.13, bf16[2,1024,256]{1,2,0:T(8,128)(2,1)} %collective-permute-done.3, bf16[1,1024,256]{1,2,0:T(8,128)(2,1)S(1)} %slice.19, pred[]{:T(512)S(6)} %ge.7), kind=kOutput, calls=%fused_computation | convolution fusion | flops 537395200 | bytes 4718593 | tf_op jit(solution)/shard_map/jrk,jkc->jrc/dot_general | solution.py:26
  192.8 0.8 fusion.54
  193.6 1.0 copy.12
  (20 shorter events, 0.2 us)
Async XLA Ops:
  6.5 34.1 %copy-start = (bf16[2,1,512,1024]{3,2,1,0:T(8,128)(2,1)S(1)}, bf16[2,1,512,1024]{3,2,1,0:T(8,128)(2,1)}, u32[]{:S(2)}) copy-start(bf16[2,1,512,1024]{3,2,1,0:T(8,128)(2,1)} %param.8) | copy-start | bytes 6291460
  6.5 34.1 %all-gather.12.cloned.1.call-start = ((), (), s32[]{:S(2)}) async-start(), calls=%async_computation.3 | async-start | bytes 1572864 | tf_op jit(solution)/shard_map/all_gather | solution.py:30
  7.3 65.6 %copy-start.1 = (bf16[2,1,512,256]{3,2,1,0:T(8,128)(2,1)S(1)}, bf16[2,1,512,256]{3,2,1,0:T(8,128)(2,1)}, u32[]{:S(2)}) copy-start(bf16[2,1,512,256]{3,2,1,0:T(8,128)(2,1)} %param.7) | copy-start | bytes 1572868
  7.3 63.6 %all-gather.6.cloned.1.call-start = ((), (), s32[]{:S(2)}) async-start(), calls=%async_computation | async-start | bytes 1572864 | tf_op jit(solution)/shard_map/all_gather | solution.py:33
  43.4 81.3 %all-gather.8.cloned.1.call-start = ((), (), s32[]{:S(2)}) async-start(), calls=%async_computation.1 | async-start | bytes 1572864 | tf_op jit(solution)/shard_map/all_gather | solution.py:30
  70.9 15.0 %collective-permute-start.1 = (bf16[2,1024,256]{2,1,0:T(8,128)(2,1)}, bf16[2,1024,256]{2,1,0:T(8,128)(2,1)}, u32[]{:S(2)}, u32[]{:S(2)}) collective-permute-start(bf16[2,1024,256]{2,1,0:T(8,128)(2,1)} %all-gather.6.cloned.1.call-done), channel_id=1, source_target_pairs={{0,254},{2,0},{4,2},{6,4},{8,6},{10,8},{12,10},{14,12},{16,14},{18... | collective-permute-start | bytes 3145736 | tf_op jit(solution)/shard_map/ppermute | solution.py:10
  71.7 15.3 %collective-permute-start = (bf16[2,1024,256]{2,1,0:T(8,128)(2,1)}, bf16[2,1024,256]{2,1,0:T(8,128)(2,1)}, u32[]{:S(2)}, u32[]{:S(2)}) collective-permute-start(bf16[2,1024,256]{2,1,0:T(8,128)(2,1)} %all-gather.6.cloned.1.call-done), channel_id=1, source_target_pairs={{0,2},{2,4},{4,6},{6,8},{8,10},{10,12},{12,14},{14,16},{16,18},{18... | collective-permute-start | bytes 3145736 | tf_op jit(solution)/shard_map/ppermute | solution.py:10
  88.1 3.0 %copy-start.4 = (bf16[2,1,512,1024]{3,2,1,0:T(8,128)(2,1)S(1)}, bf16[2,1,512,1024]{3,2,1,0:T(8,128)(2,1)}, u32[]{:S(2)}) copy-start(bf16[2,1,512,1024]{3,2,1,0:T(8,128)(2,1)} %param.9) | copy-start | bytes 6291460
  94.2 61.5 %all-gather.10.cloned.1.call-start = ((), (), s32[]{:S(2)}) async-start(), calls=%async_computation.2 | async-start | bytes 1572864 | tf_op jit(solution)/shard_map/all_gather | solution.py:33
  155.7 27.2 %collective-permute-start.3 = (bf16[2,1024,256]{1,2,0:T(8,128)(2,1)}, bf16[2,1024,256]{1,2,0:T(8,128)(2,1)}, u32[]{:S(2)}, u32[]{:S(2)}) collective-permute-start(bf16[2,1024,256]{1,2,0:T(8,128)(2,1)} %all-gather.10.cloned.1.call-done), channel_id=1, source_target_pairs={{0,252},{2,254},{4,0},{6,2},{8,4},{10,6},{12,8},{14,10},{16,12},{1... | collective-permute-start | bytes 3145736 | tf_op jit(solution)/shard_map/ppermute | solution.py:10
  161.0 28.0 %collective-permute-start.2 = (bf16[2,1024,256]{1,2,0:T(8,128)(2,1)}, bf16[2,1024,256]{1,2,0:T(8,128)(2,1)S(1)}, u32[]{:S(2)}, u32[]{:S(2)}) collective-permute-start(bf16[2,1024,256]{1,2,0:T(8,128)(2,1)} %all-gather.10.cloned.1.call-done), channel_id=1, source_target_pairs={{0,4},{2,6},{4,8},{6,10},{8,12},{10,14},{12,16},{14,18},{16,20},{1... | collective-permute-start | bytes 3145736 | tf_op jit(solution)/shard_map/ppermute | solution.py:10
  189.0 1.0 copy-start.3
  190.0 2.8 %copy-start.2 = (bf16[2,512,256]{1,2,0:T(8,128)(2,1)S(1)}, bf16[2,512,256]{1,2,0:T(8,128)(2,1)}, u32[]{:S(2)}) copy-start(bf16[2,512,256]{1,2,0:T(8,128)(2,1)} %fusion.33) | copy-start | bytes 1572868
  190.0 2.8 %copy-start.5 = (bf16[2,1,512,1024]{3,2,1,0:T(8,128)(2,1)S(1)}, bf16[2,1,512,1024]{3,2,1,0:T(8,128)(2,1)}, u32[]{:S(2)}) copy-start(bf16[2,1,512,1024]{3,2,1,0:T(8,128)(2,1)} %param.12) | copy-start | bytes 6291460
Sparse Core Ops, SparseCore 0:
  9.1 31.4 all-gather.11
  43.5 27.3 all-gather.5
  94.4 30.3 all-gather.7
  128.4 27.3 all-gather.9
where the time goes:
time: 201 us
  waiting for transfers between devices  159 us (79%)
  matrix products  15.9 us (8%)
  between operations  13.2 us (7%)
  starting transfers between devices  7.28 us (4%)
  local copies, waits for them, and re-layouts  5.44 us (3%)
    all_gather x2, waiting for transfers between devices, reduce_level(): lax.all_gather(forcing_now, 'row', axis=1, tiled=True)  63.8 us
    all_gather x2, waiting for transfers between devices, reduce_level(): gathered = lax.all_gather(scaled, 'row', axis=1, tiled=True)  54.9 us
    ppermute x4, waiting for transfers between devices, from_behind(): return lax.ppermute(value, axis, pairs)  39.8 us
    dot_general x6, matrix products, product(): jnp.einsum('jrk,jkc->jrc', blocks, vectors, preferred_element_type=jnp.fl...  15.9 us
    ppermute x4, starting transfers between devices, from_behind(): return lax.ppermute(value, axis, pairs)  7.15 us
  transfers between devices with their start and end apart: 8, of which 7 were waited for; matrix products, arithmetic and copies ran while one was open for 1% of the time, Pallas kernels for 0%

commit v1 on v0

v1 whole, which is shorter than its diff:
```python
import jax
import jax.numpy as jnp
from jax import lax
from jax.experimental import pallas as pl
from jax.experimental.pallas import tpu as pltpu
from jax.sharding import PartitionSpec as P

FIRST_PIECES, MID_PIECES, LAST_PIECES = 2, 2, 2


def shift(value, steps):
    count = lax.axis_size("st")
    pairs = [(source, (source + steps) % count) for source in range(count)]
    return lax.ppermute(value, "st", pairs)


def shift_across(value, steps):
    count = lax.axis_size("st")
    pairs = [
        (2 * source + row, 2 * ((source + steps) % count) + 1 - row)
        for source in range(count)
        for row in range(2)
    ]
    return lax.ppermute(value, ("st", "row"), pairs)


def swap(value):
    return lax.ppermute(value, "row", [(0, 1), (1, 0)])


def dot(a, b):
    return jnp.dot(a, b, preferred_element_type=jnp.float32)


def half_of(block, j, which):
    half = block.shape[-1] // 2
    return block[j, 0, :, pl.ds(pl.multiple_of(which * half, half), half)]


def side_by_side(refs, j):
    values = [ref[j] for ref in refs]
    return values[0] if len(values) == 1 else jnp.concatenate(values, axis=-1)


def call(kernel, where, operands, outs, flops):
    moved = sum(o.size * o.dtype.itemsize for o in operands) + sum(
        o.size * o.dtype.itemsize for o in outs
    )
    return pl.pallas_call(
        kernel,
        out_shape=outs,
        in_specs=[pl.BlockSpec(memory_space=pltpu.SMEM)]
        + [pl.BlockSpec(memory_space=pltpu.VMEM)] * len(operands),
        out_specs=[pl.BlockSpec(memory_space=pltpu.VMEM)] * len(outs),
        compiler_params=pltpu.CompilerParams(vmem_limit_bytes=32 * 2**20),
        cost_estimate=pl.CostEstimate(flops=flops, bytes_accessed=moved, transcendentals=0),
    )(where, *operands)


def scale_own_kernel(where, inverse, *refs):
    own, out = refs[:-1], refs[-1]
    for j in range(inverse.shape[0]):
        out[j] = dot(half_of(inverse, j, where[0]), side_by_side(own, j))


def scale_other_kernel(count, where, inverse, part, *refs):
    other, outs = refs[:count], refs[count:]
    for j in range(inverse.shape[0]):
        total = part[j] + dot(half_of(inverse, j, 1 - where[0]), side_by_side(other, j))
        total = total.astype(jnp.bfloat16)
        width = outs[0].shape[-1]
        for c, out in enumerate(outs):
            out[j] = total[:, c * width : (c + 1) * width]


def scale(where, inverse, own, other, pieces):
    stations, _, rows, wide = inverse.shape
    columns = sum(o.shape[-1] for o in own)
    flops = stations * rows * wide * columns
    part = call(
        scale_own_kernel, where, [inverse, *own],
        [jax.ShapeDtypeStruct((stations, rows, columns), jnp.float32)], flops,
    )[0]
    outs = [jax.ShapeDtypeStruct((stations, rows, columns // pieces), jnp.bfloat16)] * pieces
    return call(
        lambda *refs: scale_other_kernel(len(other), *refs), where,
        [inverse, part, *other], outs, flops,
    )


def couple_both(where, lower, upper, below, above, j, stations, which):
    below_at = jnp.maximum(j - where[1], 0)
    above_at = jnp.minimum(j + where[2], stations - 1)
    low = dot(half_of(lower, j, which), below[below_at])
    high = dot(half_of(upper, j, which), above[above_at])
    if j == 0:
        low = jnp.where(where[1] == 0, low, 0.0)
    if j == stations - 1:
        high = jnp.where(where[2] == 0, high, 0.0)
    return low + high


def couple_own_kernel(start, where, lower, upper, below, above, now, out):
    stations = lower.shape[0]
    width = out.shape[-1]
    for j in range(stations):
        coupled = couple_both(where, lower, upper, below, above, j, stations, where[0])
        out[j] = now[j][:, start : start + width].astype(jnp.float32) - coupled


def couple_other_kernel(where, lower, upper, below, above, part, *outs):
    stations = lower.shape[0]
    width = outs[0].shape[-1]
    for j in range(stations):
        coupled = couple_both(where, lower, upper, below, above, j, stations, 1 - where[0])
        total = (part[j] - coupled).astype(outs[0].dtype)
        for c, out in enumerate(outs):
            out[j] = total[:, c * width : (c + 1) * width]


def couple_last_kernel(where, lower, upper, below, above, part, *rest):
    out = rest[-1]
    stations = lower.shape[0]
    for j in range(stations):
        @pl.when(pl.program_id(0) == j)
        def _():
            coupled = couple_both(where, lower, upper, below, above, j, stations, 1 - where[0])
            out[...] = (part[j] - coupled).astype(out.dtype)


def on_device(forcing, inv1, low1, up1, inv2, low2, up2):
    stations, _, rows, columns = forcing.shape
    wide = inv1.shape[-1]
    piece = columns // LAST_PIECES
    middle = columns // MID_PIECES
    row = lax.axis_index("row")
    position = lax.axis_index("st")
    count = lax.axis_size("st")

    def where_for(stride):
        wraps = [position < stride, position >= count - stride]
        return jnp.stack([row] + [flag.astype(jnp.int32) for flag in wraps])

    where1, where2 = where_for(1), where_for(2)

    def array(width, dtype=jnp.bfloat16):
        return jax.ShapeDtypeStruct((stations, rows, width), dtype)

    def flops(width):
        return 2 * stations * rows * wide * width

    def spread(scaled, stride):
        def send(move, steps):
            return move(scaled, steps)

        across = send(shift_across, stride), send(shift_across, -stride)
        straight = send(shift, stride), send(shift, -stride)
        return straight, across

    def own_part(where, lower, upper, straight, now, start):
        width = straight[0].shape[-1]
        return call(
            lambda *refs: couple_own_kernel(start, *refs), where,
            [lower, upper, *straight, now], [array(width, jnp.float32)], flops(width),
        )[0]

    flat = forcing.reshape(stations, rows, columns)
    if FIRST_PIECES == 1:
        scaled1 = scale(where1, inv1, [flat], [swap(flat)], MID_PIECES)
    else:
        scaled1 = []
        for c in range(MID_PIECES):
            mine = flat[:, :, c * middle : (c + 1) * middle]
            scaled1 += scale(where1, inv1, [mine], [swap(mine)], 1)
    firsts = []
    for c in range(MID_PIECES):
        straight, across = spread(scaled1[c], 1)
        part = own_part(where1, low1, up1, straight, flat, c * middle)
        firsts += call(
            couple_other_kernel, where1, [low1, up1, *across, part],
            [array(piece)] * (LAST_PIECES // MID_PIECES), flops(middle),
        )
    out = None
    for c in range(LAST_PIECES):
        first = firsts[c]
        other = swap(first)
        (scaled2,) = scale(where2, inv2, [first], [other], 1)
        straight, across = spread(scaled2, 2)
        part = own_part(where2, low2, up2, straight, first, 0)
        operands = [where2, low2, up2, *across, part]
        specs = [pl.BlockSpec(memory_space=pltpu.SMEM)]
        specs += [pl.BlockSpec(memory_space=pltpu.VMEM)] * 5
        aliases = {}
        if out is not None:
            aliases = {len(operands): 0}
            operands.append(out)
            specs.append(pl.BlockSpec(memory_space=pl.ANY))
        run = pl.pallas_call(
            couple_last_kernel,
            grid=(stations,),
            out_shape=jax.ShapeDtypeStruct(forcing.shape, forcing.dtype),
            in_specs=specs,
            out_specs=pl.BlockSpec((None, None, rows, piece), lambda j, c=c: (j, 0, 0, c)),
            input_output_aliases=aliases,
            compiler_params=pltpu.CompilerParams(vmem_limit_bytes=32 * 2**20),
            cost_estimate=pl.CostEstimate(
                flops=flops(piece), bytes_accessed=4 * stations * rows * wide, transcendentals=0
            ),
            name="couple_last",
        )
        out = run(*operands)
    return out


def solution(mesh):
    spec = P(None, "st", "row", None)

    return jax.shard_map(
        on_device, mesh=mesh, in_specs=(spec,) * 7, out_specs=spec, check_vma=False
    )
```

time: 201 us -> 103 us (0.51)
  waiting for transfers between devices: 159 us -> 10.1 us
  starting transfers between devices: 7.28 us -> 69.1 us
  Pallas kernels: 0 us -> 19.6 us
  matrix products: 15.9 us -> 0 us
  between operations: 13.2 us -> 0.23 us
  local copies, waits for them, and re-layouts: 5.44 us -> 2.69 us
    all_gather x4 -> x0, waiting for transfers between devices: 119 us -> none  [the longest x2 63.8 us: reduce_level(): lax.all_gather(forcing_now, 'row', axis=1, tiled=True)]
    ppermute x4 -> x20, starting transfers between devices: 7.15 us -> 69.1 us  [the longest x8 33.8 us: shift(): return lax.ppermute(value, 'st', pairs)]
    ppermute x4 -> x20, waiting for transfers between devices: 39.8 us -> 10.1 us  [the longest x8 7.8 us: shift_across(): return lax.ppermute(value, ('st', 'row'), pairs)]
    pallas_call x0 -> x16, Pallas kernels: none -> 19.6 us  [the longest x14 15.3 us: call(): pl.pallas_call(kernel, out_shape=outs, in_specs=[pl.BlockSpec(memory_spac...]
    dot_general x6 -> x0, matrix products: 15.9 us -> none  [product(): jnp.einsum('jrk,jkc->jrc', blocks, vectors, preferred_element_type=jnp.fl...]
    slice x4 -> x1, local copies, waits for them, and re-layouts: 3.26 us -> 1.06 us  [on_device(): mine = flat[:, :, c * middle:(c + 1) * middle]]
  transfers between devices with their start and end apart: 8 -> 20, of which waited for: 7 -> 4; matrix products, arithmetic and copies ran while one was open for 1% -> 0% of each run, Pallas kernels for 0% -> 17%
where the time goes in v1:
time: 103 us; the launch traced here: 102 us
  starting transfers between devices  69.1 us (67%)
  Pallas kernels  19.6 us (19%)
  waiting for transfers between devices  10.1 us (10%)
  local copies, waits for them, and re-layouts  2.69 us (3%)
    ppermute x8, starting transfers between devices, shift(): return lax.ppermute(value, 'st', pairs)  33.8 us
    ppermute x8, starting transfers between devices, shift_across(): return lax.ppermute(value, ('st', 'row'), pairs)  25.8 us
    pallas_call x14, Pallas kernels, call(): pl.pallas_call(kernel, out_shape=outs, in_specs=[pl.BlockSpec(memory_spac...  15.3 us
    ppermute x4, starting transfers between devices, swap(): return lax.ppermute(value, 'row', [(0, 1), (1, 0)])  9.53 us
    ppermute x8, waiting for transfers between devices, shift_across(): return lax.ppermute(value, ('st', 'row'), pairs)  7.8 us
    pallas_call x2, Pallas kernels, on_device(): out = run(*operands)  4.26 us
    ppermute x4, waiting for transfers between devices, swap(): return lax.ppermute(value, 'row', [(0, 1), (1, 0)])  2.26 us
  transfers between devices with their start and end apart: 20, of which 4 were waited for; matrix products, arithmetic and copies ran while one was open for 0% of the time, Pallas kernels for 17%

profile of v1, /device:TPU:1, one launch (start us, length us, event | category | flops | bytes accessed | tf_op | source)
XLA Modules:
  0.0 101.8 jit_solution(14423339990301129733)
XLA Ops:
  1.1 3.6 %collective-permute-start.10 = (bf16[2,512,128]{2,1,0:T(8,128)(2,1)S(1)}, bf16[2,512,128]{2,1,0:T(8,128)(2,1)S(1)}, u32[]{:S(2)}, u32[]{:S(2)}) collective-permute-start(bf16[2,512,128]{2,1,0:T(8,128)(2,1)S(1)} %get-tuple-element.5.refs_0_), channel_id=1, source_target_pairs={{0,1},{1,0},{2,3},{3,2},{4,5},{5,4},{6,7},{7,6},{8,9},{9,8},{10,11... | collective-permute-start | bytes 786440 | tf_op jit(solution)/shard_map/ppermute | solution.py:28
  4.9 1.6 %copy-done.4 = bf16[2,1,512,1024]{3,2,1,0:T(8,128)(2,1)S(1)} copy-done((bf16[2,1,512,1024]{3,2,1,0:T(8,128)(2,1)S(1)}, bf16[2,1,512,1024]{3,2,1,0:T(8,128)(2,1)}, u32[]{:S(2)}) %copy-start.4) | copy-done | bytes 2097176
  7.5 2.3 %collective-permute-done.10.refs_3_ = bf16[2,512,128]{2,1,0:T(8,128)(2,1)S(1)} collective-permute-done((bf16[2,512,128]{2,1,0:T(8,128)(2,1)S(1)}, bf16[2,512,128]{2,1,0:T(8,128)(2,1)S(1)}, u32[]{:S(2)}, u32[]{:S(2)}) %collective-permute-start.10) | collective-permute-done | bytes 262176 | tf_op jit(solution)/shard_map/ppermute | solution.py:28
  10.7 4.9 %collective-permute-start.13 = (bf16[2,512,128]{2,1,0:T(8,128)(2,1)S(1)}, bf16[2,512,128]{2,1,0:T(8,128)(2,1)S(1)}, u32[]{:S(2)}, u32[]{:S(2)}) collective-permute-start(bf16[2,512,128]{2,1,0:T(8,128)(2,1)S(1)} %shard_map.81), channel_id=1, source_target_pairs={{0,2},{2,4},{4,6},{6,8},{8,10},{10,12},{12,14},{14,16},{16,18},{18... | collective-permute-start | bytes 786440 | tf_op jit(solution)/shard_map/ppermute | solution.py:14
  16.1 3.7 %collective-permute-start.11 = (bf16[2,512,128]{2,1,0:T(8,128)(2,1)S(1)}, bf16[2,512,128]{2,1,0:T(8,128)(2,1)S(1)}, u32[]{:S(2)}, u32[]{:S(2)}) collective-permute-start(bf16[2,512,128]{2,1,0:T(8,128)(2,1)S(1)} %shard_map.81), channel_id=1, source_target_pairs={{0,3},{1,2},{2,5},{3,4},{4,7},{5,6},{6,9},{7,8},{8,11},{9,10},{10,... | collective-permute-start | bytes 786440 | tf_op jit(solution)/shard_map/ppermute | solution.py:24
  19.8 3.7 %collective-permute-start.12 = (bf16[2,512,128]{2,1,0:T(8,128)(2,1)S(1)}, bf16[2,512,128]{2,1,0:T(8,128)(2,1)S(1)}, u32[]{:S(2)}, u32[]{:S(2)}) collective-permute-start(bf16[2,512,128]{2,1,0:T(8,128)(2,1)S(1)} %shard_map.81), channel_id=1, source_target_pairs={{0,255},{1,254},{2,1},{3,0},{4,3},{5,2},{6,5},{7,4},{8,7},{9,6},{1... | collective-permute-start | bytes 786440 | tf_op jit(solution)/shard_map/ppermute | solution.py:24
  25.6 5.7 %collective-permute-start.4 = (bf16[2,512,128]{2,1,0:T(8,128)(2,1)S(1)}, bf16[2,512,128]{2,1,0:T(8,128)(2,1)S(1)}, u32[]{:S(2)}, u32[]{:S(2)}) collective-permute-start(bf16[2,512,128]{2,1,0:T(8,128)(2,1)S(1)} %shard_map.74), channel_id=1, source_target_pairs={{0,254},{2,0},{4,2},{6,4},{8,6},{10,8},{12,10},{14,12},{16,14},{18... | collective-permute-start | bytes 786440 | tf_op jit(solution)/shard_map/ppermute | solution.py:14
  31.3 1.7 %collective-permute-done.11.below = bf16[2,512,128]{2,1,0:T(8,128)(2,1)S(1)} collective-permute-done((bf16[2,512,128]{2,1,0:T(8,128)(2,1)S(1)}, bf16[2,512,128]{2,1,0:T(8,128)(2,1)S(1)}, u32[]{:S(2)}, u32[]{:S(2)}) %collective-permute-start.11) | collective-permute-done | bytes 262176 | tf_op jit(solution)/shard_map/ppermute | solution.py:24
  33.0 4.6 %collective-permute-start.2 = (bf16[2,512,128]{2,1,0:T(8,128)(2,1)S(1)}, bf16[2,512,128]{2,1,0:T(8,128)(2,1)S(1)}, u32[]{:S(2)}, u32[]{:S(2)}) collective-permute-start(bf16[2,512,128]{2,1,0:T(8,128)(2,1)S(1)} %shard_map.74), channel_id=1, source_target_pairs={{0,255},{1,254},{2,1},{3,0},{4,3},{5,2},{6,5},{7,4},{8,7},{9,6},{1... | collective-permute-start | bytes 786440 | tf_op jit(solution)/shard_map/ppermute | solution.py:24
  37.6 1.3 %shard_map.82.part = f32[2,512,128]{2,1,0:T(8,128)S(1)} custom-call(s32[3]{0:T(128)S(1)} %pad_add_fusion.1.where.refs_0_, bf16[2,1,512,1024]{3,2,1,0:T(8,128)(2,1)S(1)} %copy-done, bf16[2,1,512,1024]{3,2,1,0:T(8,128)(2,1)S(1)} %copy-done.1, bf16[2,512,128]{2,1,0:T(8,128)(2,1)S(1)} %collective-permute-done.13.refs_3_, ...), custom_call_target="tpu_custom_call" | custom-call | flops 268435456 | bytes 5767168 | tf_op jit(solution)/shard_map/pallas_call | solution.py:49
  38.9 1.3 %shard_map.83.refs_0_.refs_5_ = bf16[2,512,128]{2,1,0:T(8,128)(2,1)S(1)} custom-call(s32[3]{0:T(128)S(1)} %pad_add_fusion.1.where.refs_0_, bf16[2,1,512,1024]{3,2,1,0:T(8,128)(2,1)S(1)} %copy-done, bf16[2,1,512,1024]{3,2,1,0:T(8,128)(2,1)S(1)} %copy-done.1, bf16[2,512,128]{2,1,0:T(8,128)(2,1)S(1)} %collective-permute-done.11.below, ...), custom_call_target="tpu_custom_call" | custom-call | flops 268435456 | bytes 5505024 | tf_op jit(solution)/shard_map/pallas_call | solution.py:49
  40.1 2.6 %collective-permute-start.15 = (bf16[2,512,128]{2,1,0:T(8,128)(2,1)S(1)}, bf16[2,512,128]{2,1,0:T(8,128)(2,1)S(1)}, u32[]{:S(2)}, u32[]{:S(2)}) collective-permute-start(bf16[2,512,128]{2,1,0:T(8,128)(2,1)S(1)} %shard_map.83.refs_0_.refs_5_), channel_id=1, source_target_pairs={{0,1},{1,0},{2,3},{3,2},{4,5},{5,4},{6,7},{7,6},{8,9},{9,8},{10,11... | collective-permute-start | bytes 786440 | tf_op jit(solution)/shard_map/ppermute | solution.py:28
  42.8 1.3 %shard_map.75.part = f32[2,512,128]{2,1,0:T(8,128)S(1)} custom-call(s32[3]{0:T(128)S(1)} %pad_add_fusion.1.where.refs_0_, bf16[2,1,512,1024]{3,2,1,0:T(8,128)(2,1)S(1)} %copy-done, bf16[2,1,512,1024]{3,2,1,0:T(8,128)(2,1)S(1)} %copy-done.1, bf16[2,512,128]{2,1,0:T(8,128)(2,1)S(1)} %collective-permute-done.3.refs_3_, ...), custom_call_target="tpu_custom_call" | custom-call | flops 268435456 | bytes 5767168 | tf_op jit(solution)/shard_map/pallas_call | solution.py:49
  44.1 1.3 %shard_map.76.refs_0_.refs_5_ = bf16[2,512,128]{2,1,0:T(8,128)(2,1)S(1)} custom-call(s32[3]{0:T(128)S(1)} %pad_add_fusion.1.where.refs_0_, bf16[2,1,512,1024]{3,2,1,0:T(8,128)(2,1)S(1)} %copy-done, bf16[2,1,512,1024]{3,2,1,0:T(8,128)(2,1)S(1)} %copy-done.1, bf16[2,512,128]{2,1,0:T(8,128)(2,1)S(1)} %collective-permute-done.1.below, ...), custom_call_target="tpu_custom_call" | custom-call | flops 268435456 | bytes 5505024 | tf_op jit(solution)/shard_map/pallas_call | solution.py:49
  45.3 3.2 %collective-permute-start.5 = (bf16[2,512,128]{2,1,0:T(8,128)(2,1)S(1)}, bf16[2,512,128]{2,1,0:T(8,128)(2,1)S(1)}, u32[]{:S(2)}, u32[]{:S(2)}) collective-permute-start(bf16[2,512,128]{2,1,0:T(8,128)(2,1)S(1)} %shard_map.76.refs_0_.refs_5_), channel_id=1, source_target_pairs={{0,1},{1,0},{2,3},{3,2},{4,5},{5,4},{6,7},{7,6},{8,9},{9,8},{10,11... | collective-permute-start | bytes 786440 | tf_op jit(solution)/shard_map/ppermute | solution.py:28
  51.6 11.0 %collective-permute-start.19 = (bf16[2,512,128]{2,1,0:T(8,128)(2,1)S(1)}, bf16[2,512,128]{2,1,0:T(8,128)(2,1)S(1)}, u32[]{:S(2)}, u32[]{:S(2)}) collective-permute-start(bf16[2,512,128]{2,1,0:T(8,128)(2,1)S(1)} %shard_map.85), channel_id=1, source_target_pairs={{0,252},{2,254},{4,0},{6,2},{8,4},{10,6},{12,8},{14,10},{16,12},{1... | collective-permute-start | bytes 786440 | tf_op jit(solution)/shard_map/ppermute | solution.py:14
  63.7 11.4 %collective-permute-start.9 = (bf16[2,512,128]{2,1,0:T(8,128)(2,1)S(1)}, bf16[2,512,128]{2,1,0:T(8,128)(2,1)S(1)}, u32[]{:S(2)}, u32[]{:S(2)}) collective-permute-start(bf16[2,512,128]{2,1,0:T(8,128)(2,1)S(1)} %shard_map.78), channel_id=1, source_target_pairs={{0,252},{2,254},{4,0},{6,2},{8,4},{10,6},{12,8},{14,10},{16,12},{1... | collective-permute-start | bytes 786440 | tf_op jit(solution)/shard_map/ppermute | solution.py:14
  75.1 6.9 %collective-permute-start.17 = (bf16[2,512,128]{2,1,0:T(8,128)(2,1)S(1)}, bf16[2,512,128]{2,1,0:T(8,128)(2,1)S(1)}, u32[]{:S(2)}, u32[]{:S(2)}) collective-permute-start(bf16[2,512,128]{2,1,0:T(8,128)(2,1)S(1)} %shard_map.85), channel_id=1, source_target_pairs={{0,253},{1,252},{2,255},{3,254},{4,1},{5,0},{6,3},{7,2},{8,5},{9,4... | collective-permute-start | bytes 786440 | tf_op jit(solution)/shard_map/ppermute | solution.py:24
  82.0 6.9 %collective-permute-start.7 = (bf16[2,512,128]{2,1,0:T(8,128)(2,1)S(1)}, bf16[2,512,128]{2,1,0:T(8,128)(2,1)S(1)}, u32[]{:S(2)}, u32[]{:S(2)}) collective-permute-start(bf16[2,512,128]{2,1,0:T(8,128)(2,1)S(1)} %shard_map.78), channel_id=1, source_target_pairs={{0,253},{1,252},{2,255},{3,254},{4,1},{5,0},{6,3},{7,2},{8,5},{9,4... | collective-permute-start | bytes 786440 | tf_op jit(solution)/shard_map/ppermute | solution.py:24
  88.9 1.3 %shard_map.86.part = f32[2,512,128]{2,1,0:T(8,128)S(1)} custom-call(s32[3]{0:T(128)S(1)} %pad_add_fusion.where.refs_0_, bf16[2,1,512,1024]{3,2,1,0:T(8,128)(2,1)S(1)} %copy-done.2, bf16[2,1,512,1024]{3,2,1,0:T(8,128)(2,1)S(1)} %copy-done.3, bf16[2,512,128]{2,1,0:T(8,128)(2,1)S(1)} %collective-permute-done.18.refs_3_, ...), custom_call_target="tpu_custom_call" | custom-call | flops 268435456 | bytes 5505024 | tf_op jit(solution)/shard_map/pallas_call | solution.py:49
  90.2 1.3 %shard_map.79.part = f32[2,512,128]{2,1,0:T(8,128)S(1)} custom-call(s32[3]{0:T(128)S(1)} %pad_add_fusion.where.refs_0_, bf16[2,1,512,1024]{3,2,1,0:T(8,128)(2,1)S(1)} %copy-done.2, bf16[2,1,512,1024]{3,2,1,0:T(8,128)(2,1)S(1)} %copy-done.3, bf16[2,512,128]{2,1,0:T(8,128)(2,1)S(1)} %collective-permute-done.8.refs_3_, ...), custom_call_target="tpu_custom_call" | custom-call | flops 268435456 | bytes 5505024 | tf_op jit(solution)/shard_map/pallas_call | solution.py:49
  92.3 2.1 %couple_last.2.rest_0_ = bf16[2,1,512,256]{3,2,1,0:T(8,128)(2,1)} custom-call(s32[3]{0:T(128)S(1)} %pad_add_fusion.where.refs_0_, bf16[2,1,512,1024]{3,2,1,0:T(8,128)(2,1)S(1)} %copy-done.2, bf16[2,1,512,1024]{3,2,1,0:T(8,128)(2,1)S(1)} %copy-done.3, bf16[2,512,128]{2,1,0:T(8,128)(2,1)S(1)} %collective-permute-done.16.below, ...), custom_call_target="tpu_custom_call" | custom-call | flops 268435456 | bytes 4194304 | tf_op jit(solution)/shard_map/couple_last/pallas_call | solution.py:211
  94.4 5.3 %collective-permute-done.6.below = bf16[2,512,128]{2,1,0:T(8,128)(2,1)S(1)} collective-permute-done((bf16[2,512,128]{2,1,0:T(8,128)(2,1)S(1)}, bf16[2,512,128]{2,1,0:T(8,128)(2,1)S(1)}, u32[]{:S(2)}, u32[]{:S(2)}) %collective-permute-start.6) | collective-permute-done | bytes 262176 | tf_op jit(solution)/shard_map/ppermute | solution.py:24
  99.7 2.1 %couple_last.3 = bf16[2,1,512,256]{3,2,1,0:T(8,128)(2,1)} custom-call(s32[3]{0:T(128)S(1)} %pad_add_fusion.where.refs_0_, bf16[2,1,512,1024]{3,2,1,0:T(8,128)(2,1)S(1)} %copy-done.2, bf16[2,1,512,1024]{3,2,1,0:T(8,128)(2,1)S(1)} %copy-done.3, bf16[2,512,128]{2,1,0:T(8,128)(2,1)S(1)} %collective-permute-done.6.below, ...), custom_call_target="tpu_custom_call", output_to_operand_aliasing={{}: (6, {})} | custom-call | flops 268435456 | bytes 4194304 | tf_op jit(solution)/shard_map/couple_last/pallas_call | solution.py:211
  (49 shorter events, 10.8 us)
Async XLA Ops:
  1.1 8.6 %collective-permute-start.10 = (bf16[2,512,128]{2,1,0:T(8,128)(2,1)S(1)}, bf16[2,512,128]{2,1,0:T(8,128)(2,1)S(1)}, u32[]{:S(2)}, u32[]{:S(2)}) collective-permute-start(bf16[2,512,128]{2,1,0:T(8,128)(2,1)S(1)} %get-tuple-element.5.refs_0_), channel_id=1, source_target_pairs={{0,1},{1,0},{2,3},{3,2},{4,5},{5,4},{6,7},{7,6},{8,9},{9,8},{10,11... | collective-permute-start | bytes 786440 | tf_op jit(solution)/shard_map/ppermute | solution.py:28
  4.7 19.8 %collective-permute-start = (bf16[2,512,128]{2,1,0:T(8,128)(2,1)S(1)}, bf16[2,512,128]{2,1,0:T(8,128)(2,1)S(1)}, u32[]{:S(2)}, u32[]{:S(2)}) collective-permute-start(bf16[2,512,128]{2,1,0:T(8,128)(2,1)S(1)} %get-tuple-element.6.refs_0_), channel_id=1, source_target_pairs={{0,1},{1,0},{2,3},{3,2},{4,5},{5,4},{6,7},{7,6},{8,9},{9,8},{10,11... | collective-permute-start | bytes 786440 | tf_op jit(solution)/shard_map/ppermute | solution.py:28
  10.7 14.9 %collective-permute-start.13 = (bf16[2,512,128]{2,1,0:T(8,128)(2,1)S(1)}, bf16[2,512,128]{2,1,0:T(8,128)(2,1)S(1)}, u32[]{:S(2)}, u32[]{:S(2)}) collective-permute-start(bf16[2,512,128]{2,1,0:T(8,128)(2,1)S(1)} %shard_map.81), channel_id=1, source_target_pairs={{0,2},{2,4},{4,6},{6,8},{8,10},{10,12},{12,14},{14,16},{16,18},{18... | collective-permute-start | bytes 786440 | tf_op jit(solution)/shard_map/ppermute | solution.py:14
  15.6 15.7 %collective-permute-start.14 = (bf16[2,512,128]{2,1,0:T(8,128)(2,1)S(1)}, bf16[2,512,128]{2,1,0:T(8,128)(2,1)S(1)}, u32[]{:S(2)}, u32[]{:S(2)}) collective-permute-start(bf16[2,512,128]{2,1,0:T(8,128)(2,1)S(1)} %shard_map.81), channel_id=1, source_target_pairs={{0,254},{2,0},{4,2},{6,4},{8,6},{10,8},{12,10},{14,12},{16,14},{18... | collective-permute-start | bytes 786440 | tf_op jit(solution)/shard_map/ppermute | solution.py:14
  16.1 16.9 %collective-permute-start.11 = (bf16[2,512,128]{2,1,0:T(8,128)(2,1)S(1)}, bf16[2,512,128]{2,1,0:T(8,128)(2,1)S(1)}, u32[]{:S(2)}, u32[]{:S(2)}) collective-permute-start(bf16[2,512,128]{2,1,0:T(8,128)(2,1)S(1)} %shard_map.81), channel_id=1, source_target_pairs={{0,3},{1,2},{2,5},{3,4},{4,7},{5,6},{6,9},{7,8},{8,11},{9,10},{10,... | collective-permute-start | bytes 786440 | tf_op jit(solution)/shard_map/ppermute | solution.py:24
  19.8 19.1 %collective-permute-start.12 = (bf16[2,512,128]{2,1,0:T(8,128)(2,1)S(1)}, bf16[2,512,128]{2,1,0:T(8,128)(2,1)S(1)}, u32[]{:S(2)}, u32[]{:S(2)}) collective-permute-start(bf16[2,512,128]{2,1,0:T(8,128)(2,1)S(1)} %shard_map.81), channel_id=1, source_target_pairs={{0,255},{1,254},{2,1},{3,0},{4,3},{5,2},{6,5},{7,4},{8,7},{9,6},{1... | collective-permute-start | bytes 786440 | tf_op jit(solution)/shard_map/ppermute | solution.py:24
  23.5 14.1 %copy-start.1 = (bf16[2,1,512,1024]{3,2,1,0:T(8,128)(2,1)S(1)}, bf16[2,1,512,1024]{3,2,1,0:T(8,128)(2,1)}, u32[]{:S(2)}) copy-start(bf16[2,1,512,1024]{3,2,1,0:T(8,128)(2,1)} %upper.5) | copy-start | bytes 6291460
  24.5 13.1 %copy-start = (bf16[2,1,512,1024]{3,2,1,0:T(8,128)(2,1)S(1)}, bf16[2,1,512,1024]{3,2,1,0:T(8,128)(2,1)}, u32[]{:S(2)}) copy-start(bf16[2,1,512,1024]{3,2,1,0:T(8,128)(2,1)} %lower.5) | copy-start | bytes 6291460
  25.5 17.3 %collective-permute-start.3 = (bf16[2,512,128]{2,1,0:T(8,128)(2,1)S(1)}, bf16[2,512,128]{2,1,0:T(8,128)(2,1)S(1)}, u32[]{:S(2)}, u32[]{:S(2)}) collective-permute-start(bf16[2,512,128]{2,1,0:T(8,128)(2,1)S(1)} %shard_map.74), channel_id=1, source_target_pairs={{0,2},{2,4},{4,6},{6,8},{8,10},{10,12},{12,14},{14,16},{16,18},{18... | collective-permute-start | bytes 786440 | tf_op jit(solution)/shard_map/ppermute | solution.py:14
  25.6 17.2 %collective-permute-start.4 = (bf16[2,512,128]{2,1,0:T(8,128)(2,1)S(1)}, bf16[2,512,128]{2,1,0:T(8,128)(2,1)S(1)}, u32[]{:S(2)}, u32[]{:S(2)}) collective-permute-start(bf16[2,512,128]{2,1,0:T(8,128)(2,1)S(1)} %shard_map.74), channel_id=1, source_target_pairs={{0,254},{2,0},{4,2},{6,4},{8,6},{10,8},{12,10},{14,12},{16,14},{18... | collective-permute-start | bytes 786440 | tf_op jit(solution)/shard_map/ppermute | solution.py:14
  31.3 12.7 %collective-permute-start.1 = (bf16[2,512,128]{2,1,0:T(8,128)(2,1)S(1)}, bf16[2,512,128]{2,1,0:T(8,128)(2,1)S(1)}, u32[]{:S(2)}, u32[]{:S(2)}) collective-permute-start(bf16[2,512,128]{2,1,0:T(8,128)(2,1)S(1)} %shard_map.74), channel_id=1, source_target_pairs={{0,3},{1,2},{2,5},{3,4},{4,7},{5,6},{6,9},{7,8},{8,11},{9,10},{10,... | collective-permute-start | bytes 786440 | tf_op jit(solution)/shard_map/ppermute | solution.py:24
  33.0 11.0 %collective-permute-start.2 = (bf16[2,512,128]{2,1,0:T(8,128)(2,1)S(1)}, bf16[2,512,128]{2,1,0:T(8,128)(2,1)S(1)}, u32[]{:S(2)}, u32[]{:S(2)}) collective-permute-start(bf16[2,512,128]{2,1,0:T(8,128)(2,1)S(1)} %shard_map.74), channel_id=1, source_target_pairs={{0,255},{1,254},{2,1},{3,0},{4,3},{5,2},{6,5},{7,4},{8,7},{9,6},{1... | collective-permute-start | bytes 786440 | tf_op jit(solution)/shard_map/ppermute | solution.py:24
  40.1 9.4 %collective-permute-start.15 = (bf16[2,512,128]{2,1,0:T(8,128)(2,1)S(1)}, bf16[2,512,128]{2,1,0:T(8,128)(2,1)S(1)}, u32[]{:S(2)}, u32[]{:S(2)}) collective-permute-start(bf16[2,512,128]{2,1,0:T(8,128)(2,1)S(1)} %shard_map.83.refs_0_.refs_5_), channel_id=1, source_target_pairs={{0,1},{1,0},{2,3},{3,2},{4,5},{5,4},{6,7},{7,6},{8,9},{9,8},{10,11... | collective-permute-start | bytes 786440 | tf_op jit(solution)/shard_map/ppermute | solution.py:28
  45.3 17.3 %collective-permute-start.5 = (bf16[2,512,128]{2,1,0:T(8,128)(2,1)S(1)}, bf16[2,512,128]{2,1,0:T(8,128)(2,1)S(1)}, u32[]{:S(2)}, u32[]{:S(2)}) collective-permute-start(bf16[2,512,128]{2,1,0:T(8,128)(2,1)S(1)} %shard_map.76.refs_0_.refs_5_), channel_id=1, source_target_pairs={{0,1},{1,0},{2,3},{3,2},{4,5},{5,4},{6,7},{7,6},{8,9},{9,8},{10,11... | collective-permute-start | bytes 786440 | tf_op jit(solution)/shard_map/ppermute | solution.py:28
  50.5 24.6 %collective-permute-start.18 = (bf16[2,512,128]{2,1,0:T(8,128)(2,1)S(1)}, bf16[2,512,128]{2,1,0:T(8,128)(2,1)S(1)}, u32[]{:S(2)}, u32[]{:S(2)}) collective-permute-start(bf16[2,512,128]{2,1,0:T(8,128)(2,1)S(1)} %shard_map.85), channel_id=1, source_target_pairs={{0,4},{2,6},{4,8},{6,10},{8,12},{10,14},{12,16},{14,18},{16,20},{1... | collective-permute-start | bytes 786440 | tf_op jit(solution)/shard_map/ppermute | solution.py:14
  50.6 38.3 %copy-start.3 = (bf16[2,1,512,1024]{3,2,1,0:T(8,128)(2,1)S(1)}, bf16[2,1,512,1024]{3,2,1,0:T(8,128)(2,1)}, u32[]{:S(2)}) copy-start(bf16[2,1,512,1024]{3,2,1,0:T(8,128)(2,1)} %upper.7) | copy-start | bytes 6291460
  51.6 37.3 %copy-start.2 = (bf16[2,1,512,1024]{3,2,1,0:T(8,128)(2,1)S(1)}, bf16[2,1,512,1024]{3,2,1,0:T(8,128)(2,1)}, u32[]{:S(2)}) copy-start(bf16[2,1,512,1024]{3,2,1,0:T(8,128)(2,1)} %lower.7) | copy-start | bytes 6291460
  51.6 30.4 %collective-permute-start.19 = (bf16[2,512,128]{2,1,0:T(8,128)(2,1)S(1)}, bf16[2,512,128]{2,1,0:T(8,128)(2,1)S(1)}, u32[]{:S(2)}, u32[]{:S(2)}) collective-permute-start(bf16[2,512,128]{2,1,0:T(8,128)(2,1)S(1)} %shard_map.85), channel_id=1, source_target_pairs={{0,252},{2,254},{4,0},{6,2},{8,4},{10,6},{12,8},{14,10},{16,12},{1... | collective-permute-start | bytes 786440 | tf_op jit(solution)/shard_map/ppermute | solution.py:14
  63.6 18.4 %collective-permute-start.8 = (bf16[2,512,128]{2,1,0:T(8,128)(2,1)S(1)}, bf16[2,512,128]{2,1,0:T(8,128)(2,1)S(1)}, u32[]{:S(2)}, u32[]{:S(2)}) collective-permute-start(bf16[2,512,128]{2,1,0:T(8,128)(2,1)S(1)} %shard_map.78), channel_id=1, source_target_pairs={{0,4},{2,6},{4,8},{6,10},{8,12},{10,14},{12,16},{14,18},{16,20},{1... | collective-permute-start | bytes 786440 | tf_op jit(solution)/shard_map/ppermute | solution.py:14
  63.7 26.5 %collective-permute-start.9 = (bf16[2,512,128]{2,1,0:T(8,128)(2,1)S(1)}, bf16[2,512,128]{2,1,0:T(8,128)(2,1)S(1)}, u32[]{:S(2)}, u32[]{:S(2)}) collective-permute-start(bf16[2,512,128]{2,1,0:T(8,128)(2,1)S(1)} %shard_map.78), channel_id=1, source_target_pairs={{0,252},{2,254},{4,0},{6,2},{8,4},{10,6},{12,8},{14,10},{16,12},{1... | collective-permute-start | bytes 786440 | tf_op jit(solution)/shard_map/ppermute | solution.py:14
  75.1 17.2 %collective-permute-start.16 = (bf16[2,512,128]{2,1,0:T(8,128)(2,1)S(1)}, bf16[2,512,128]{2,1,0:T(8,128)(2,1)S(1)}, u32[]{:S(2)}, u32[]{:S(2)}) collective-permute-start(bf16[2,512,128]{2,1,0:T(8,128)(2,1)S(1)} %shard_map.85), channel_id=1, source_target_pairs={{0,5},{1,4},{2,7},{3,6},{4,9},{5,8},{6,11},{7,10},{8,13},{9,12},{1... | collective-permute-start | bytes 786440 | tf_op jit(solution)/shard_map/ppermute | solution.py:24
  75.1 17.2 %collective-permute-start.17 = (bf16[2,512,128]{2,1,0:T(8,128)(2,1)S(1)}, bf16[2,512,128]{2,1,0:T(8,128)(2,1)S(1)}, u32[]{:S(2)}, u32[]{:S(2)}) collective-permute-start(bf16[2,512,128]{2,1,0:T(8,128)(2,1)S(1)} %shard_map.85), channel_id=1, source_target_pairs={{0,253},{1,252},{2,255},{3,254},{4,1},{5,0},{6,3},{7,2},{8,5},{9,4... | collective-permute-start | bytes 786440 | tf_op jit(solution)/shard_map/ppermute | solution.py:24
  82.0 17.7 %collective-permute-start.6 = (bf16[2,512,128]{2,1,0:T(8,128)(2,1)S(1)}, bf16[2,512,128]{2,1,0:T(8,128)(2,1)S(1)}, u32[]{:S(2)}, u32[]{:S(2)}) collective-permute-start(bf16[2,512,128]{2,1,0:T(8,128)(2,1)S(1)} %shard_map.78), channel_id=1, source_target_pairs={{0,5},{1,4},{2,7},{3,6},{4,9},{5,8},{6,11},{7,10},{8,13},{9,12},{1... | collective-permute-start | bytes 786440 | tf_op jit(solution)/shard_map/ppermute | solution.py:24
  82.0 17.7 %collective-permute-start.7 = (bf16[2,512,128]{2,1,0:T(8,128)(2,1)S(1)}, bf16[2,512,128]{2,1,0:T(8,128)(2,1)S(1)}, u32[]{:S(2)}, u32[]{:S(2)}) collective-permute-start(bf16[2,512,128]{2,1,0:T(8,128)(2,1)S(1)} %shard_map.78), channel_id=1, source_target_pairs={{0,253},{1,252},{2,255},{3,254},{4,1},{5,0},{6,3},{7,2},{8,5},{9,4... | collective-permute-start | bytes 786440 | tf_op jit(solution)/shard_map/ppermute | solution.py:24
  (3 other events, 19.2 us)

commit v2 on v1

--- a/solution.py
+++ b/solution.py
@@ -88,43 +88,39 @@
     )
 
 
-def couple_both(where, lower, upper, below, above, j, stations, which):
-    below_at = jnp.maximum(j - where[1], 0)
-    above_at = jnp.minimum(j + where[2], stations - 1)
-    low = dot(half_of(lower, j, which), below[below_at])
-    high = dot(half_of(upper, j, which), above[above_at])
-    if j == 0:
-        low = jnp.where(where[1] == 0, low, 0.0)
-    if j == stations - 1:
-        high = jnp.where(where[2] == 0, high, 0.0)
-    return low + high
-
-
-def couple_own_kernel(start, where, lower, upper, below, above, now, out):
-    stations = lower.shape[0]
+def coupled_from(above, where, block, straight, across, j):
+    stations = block.shape[0]
+    if above:
+        index, edge, wraps = jnp.minimum(j + where[2], stations - 1), stations - 1, where[2]
+    else:
+        index, edge, wraps = jnp.maximum(j - where[1], 0), 0, where[1]
+    total = dot(half_of(block, j, where[0]), straight[index])
+    total += dot(half_of(block, j, 1 - where[0]), across[index])
+    return jnp.where(wraps == 0, total, 0.0) if j == edge else total
+
+
+def couple_first_kernel(above, start, where, block, straight, across, now, out):
     width = out.shape[-1]
-    for j in range(stations):
-        coupled = couple_both(where, lower, upper, below, above, j, stations, where[0])
+    for j in range(block.shape[0]):
+        coupled = coupled_from(above, where, block, straight, across, j)
         out[j] = now[j][:, start : start + width].astype(jnp.float32) - coupled
 
 
-def couple_other_kernel(where, lower, upper, below, above, part, *outs):
-    stations = lower.shape[0]
+def couple_second_kernel(above, where, block, straight, across, part, *outs):
     width = outs[0].shape[-1]
-    for j in range(stations):
-        coupled = couple_both(where, lower, upper, below, above, j, stations, 1 - where[0])
+    for j in range(block.shape[0]):
+        coupled = coupled_from(above, where, block, straight, across, j)
         total = (part[j] - coupled).astype(outs[0].dtype)
         for c, out in enumerate(outs):
             out[j] = total[:, c * width : (c + 1) * width]
 
 
-def couple_last_kernel(where, lower, upper, below, above, part, *rest):
+def couple_last_kernel(above, where, block, straight, across, part, *rest):
     out = rest[-1]
-    stations = lower.shape[0]
-    for j in range(stations):
+    for j in range(block.shape[0]):
         @pl.when(pl.program_id(0) == j)
         def _():
-            coupled = couple_both(where, lower, upper, below, above, j, stations, 1 - where[0])
+            coupled = coupled_from(above, where, block, straight, across, j)
             out[...] = (part[j] - coupled).astype(out.dtype)
 
 
@@ -153,15 +149,15 @@
         def send(move, steps):
             return move(scaled, steps)
 
-        across = send(shift_across, stride), send(shift_across, -stride)
-        straight = send(shift, stride), send(shift, -stride)
-        return straight, across
-
-    def own_part(where, lower, upper, straight, now, start):
-        width = straight[0].shape[-1]
+        below = send(shift, stride), send(shift_across, stride)
+        above = send(shift, -stride), send(shift_across, -stride)
+        return below, above
+
+    def first_part(above, where, block, pieces, now, start):
+        width = pieces[0].shape[-1]
         return call(
-            lambda *refs: couple_own_kernel(start, *refs), where,
-            [lower, upper, *straight, now], [array(width, jnp.float32)], flops(width),
+            lambda *refs: couple_first_kernel(above, start, *refs), where,
+            [block, *pieces, now], [array(width, jnp.float32)], flops(width),
         )[0]
 
     flat = forcing.reshape(stations, rows, columns)
@@ -170,14 +166,16 @@
     else:
         scaled1 = []
         for c in range(MID_PIECES):
-            mine = flat[:, :, c * middle : (c + 1) * middle]
+            source = flat if c == 0 else lax.optimization_barrier((flat, mine))[0]
+            mine = source[:, :, c * middle : (c + 1) * middle]
             scaled1 += scale(where1, inv1, [mine], [swap(mine)], 1)
     firsts = []
     for c in range(MID_PIECES):
-        straight, across = spread(scaled1[c], 1)
-        part = own_part(where1, low1, up1, straight, flat, c * middle)
+        below, above = spread(scaled1[c], 1)
+        part = first_part(True, where1, up1, above, flat, c * middle)
         firsts += call(
-            couple_other_kernel, where1, [low1, up1, *across, part],
+            lambda *refs: couple_second_kernel(False, *refs), where1,
+            [low1, *below, part],
             [array(piece)] * (LAST_PIECES // MID_PIECES), flops(middle),
         )
     out = None
@@ -185,18 +183,18 @@
         first = firsts[c]
         other = swap(first)
         (scaled2,) = scale(where2, inv2, [first], [other], 1)
-        straight, across = spread(scaled2, 2)
-        part = own_part(where2, low2, up2, straight, first, 0)
-        operands = [where2, low2, up2, *across, part]
+        below, above = spread(scaled2, 2)
+        part = first_part(False, where2, low2, below, first, 0)
+        operands = [where2, up2, *above, part]
         specs = [pl.BlockSpec(memory_space=pltpu.SMEM)]
-        specs += [pl.BlockSpec(memory_space=pltpu.VMEM)] * 5
+        specs += [pl.BlockSpec(memory_space=pltpu.VMEM)] * 4
         aliases = {}
         if out is not None:
             aliases = {len(operands): 0}
             operands.append(out)
             specs.append(pl.BlockSpec(memory_space=pl.ANY))
         run = pl.pallas_call(
-            couple_last_kernel,
+            lambda *refs: couple_last_kernel(True, *refs),
             grid=(stations,),
             out_shape=jax.ShapeDtypeStruct(forcing.shape, forcing.dtype),
             in_specs=specs,
@@ -204,7 +202,7 @@
             input_output_aliases=aliases,
             compiler_params=pltpu.CompilerParams(vmem_limit_bytes=32 * 2**20),
             cost_estimate=pl.CostEstimate(
-                flops=flops(piece), bytes_accessed=4 * stations * rows * wide, transcendentals=0
+                flops=flops(piece), bytes_accessed=2 * stations * rows * wide, transcendentals=0
             ),
             name="couple_last",
         )

time: 103 us -> 101 us (0.981)
  the two profiles are of different devices: /device:TPU:1 before, /device:TPU:123 now
where the time goes in v2:
time: 101 us
  starting transfers between devices  44.8 us (44%)
  waiting for transfers between devices  32.6 us (32%)
  Pallas kernels  19.6 us (19%)
  local copies, waits for them, and re-layouts  3.56 us (4%)
    ppermute x8, starting transfers between devices, shift_across(): return lax.ppermute(value, ('st', 'row'), pairs)  20.3 us
    ppermute x8, waiting for transfers between devices, shift_across(): return lax.ppermute(value, ('st', 'row'), pairs)  18.5 us
    ppermute x8, starting transfers between devices, shift(): return lax.ppermute(value, 'st', pairs)  17.2 us
    pallas_call x14, Pallas kernels, call(): pl.pallas_call(kernel, out_shape=outs, in_specs=[pl.BlockSpec(memory_spac...  15.3 us
    ppermute x4, waiting for transfers between devices, swap(): return lax.ppermute(value, 'row', [(0, 1), (1, 0)])  7.67 us
    ppermute x4, starting transfers between devices, swap(): return lax.ppermute(value, 'row', [(0, 1), (1, 0)])  7.26 us
    ppermute x8, waiting for transfers between devices, shift(): return lax.ppermute(value, 'st', pairs)  6.51 us
    pallas_call x2, Pallas kernels, on_device(): out = run(*operands)  4.26 us
  transfers between devices with their start and end apart: 20, of which 10 were waited for; matrix products, arithmetic and copies ran while one was open for 1% of the time, Pallas kernels for 17%

profile of v2, /device:TPU:123, one launch (start us, length us, event | category | flops | bytes accessed | tf_op | source)
XLA Modules:
  0.0 101.0 jit_solution(10909665037564225806)
XLA Ops:
  1.0 1.9 %collective-permute-start.10 = (bf16[2,512,128]{2,1,0:T(8,128)(2,1)S(1)}, bf16[2,512,128]{2,1,0:T(8,128)(2,1)S(1)}, u32[]{:S(2)}, u32[]{:S(2)}) collective-permute-start(bf16[2,512,128]{2,1,0:T(8,128)(2,1)S(1)} %slice.8.refs_0_), channel_id=1, source_target_pairs={{0,1},{1,0},{2,3},{3,2},{4,5},{5,4},{6,7},{7,6},{8,9},{9,8},{10,11... | collective-permute-start | bytes 786440 | tf_op jit(solution)/shard_map/ppermute | solution.py:28
  5.2 1.6 %copy-done = bf16[2,1,512,1024]{3,2,1,0:T(8,128)(2,1)S(1)} copy-done((bf16[2,1,512,1024]{3,2,1,0:T(8,128)(2,1)S(1)}, bf16[2,1,512,1024]{3,2,1,0:T(8,128)(2,1)}, u32[]{:S(2)}) %copy-start) | copy-done | bytes 2097176
  7.7 2.0 %collective-permute-done.10.refs_3_ = bf16[2,512,128]{2,1,0:T(8,128)(2,1)S(1)} collective-permute-done((bf16[2,512,128]{2,1,0:T(8,128)(2,1)S(1)}, bf16[2,512,128]{2,1,0:T(8,128)(2,1)S(1)}, u32[]{:S(2)}, u32[]{:S(2)}) %collective-permute-start.10) | collective-permute-done | bytes 262176 | tf_op jit(solution)/shard_map/ppermute | solution.py:28
  10.7 2.7 %collective-permute-start.13 = (bf16[2,512,128]{2,1,0:T(8,128)(2,1)S(1)}, bf16[2,512,128]{2,1,0:T(8,128)(2,1)S(1)}, u32[]{:S(2)}, u32[]{:S(2)}) collective-permute-start(bf16[2,512,128]{2,1,0:T(8,128)(2,1)S(1)} %shard_map.81), channel_id=1, source_target_pairs={{0,254},{2,0},{4,2},{6,4},{8,6},{10,8},{12,10},{14,12},{16,14},{18... | collective-permute-start | bytes 786440 | tf_op jit(solution)/shard_map/ppermute | solution.py:14
  13.5 1.8 %collective-permute-start.14 = (bf16[2,512,128]{2,1,0:T(8,128)(2,1)S(1)}, bf16[2,512,128]{2,1,0:T(8,128)(2,1)S(1)}, u32[]{:S(2)}, u32[]{:S(2)}) collective-permute-start(bf16[2,512,128]{2,1,0:T(8,128)(2,1)S(1)} %shard_map.81), channel_id=1, source_target_pairs={{0,255},{1,254},{2,1},{3,0},{4,3},{5,2},{6,5},{7,4},{8,7},{9,6},{1... | collective-permute-start | bytes 786440 | tf_op jit(solution)/shard_map/ppermute | solution.py:24
  15.3 5.4 %collective-permute-start.11 = (bf16[2,512,128]{2,1,0:T(8,128)(2,1)S(1)}, bf16[2,512,128]{2,1,0:T(8,128)(2,1)S(1)}, u32[]{:S(2)}, u32[]{:S(2)}) collective-permute-start(bf16[2,512,128]{2,1,0:T(8,128)(2,1)S(1)} %shard_map.81), channel_id=1, source_target_pairs={{0,2},{2,4},{4,6},{6,8},{8,10},{10,12},{12,14},{14,16},{16,18},{18... | collective-permute-start | bytes 786440 | tf_op jit(solution)/shard_map/ppermute | solution.py:14
  23.1 3.0 %collective-permute-start.4 = (bf16[2,512,128]{2,1,0:T(8,128)(2,1)S(1)}, bf16[2,512,128]{2,1,0:T(8,128)(2,1)S(1)}, u32[]{:S(2)}, u32[]{:S(2)}) collective-permute-start(bf16[2,512,128]{2,1,0:T(8,128)(2,1)S(1)} %shard_map.74), channel_id=1, source_target_pairs={{0,255},{1,254},{2,1},{3,0},{4,3},{5,2},{6,5},{7,4},{8,7},{9,6},{1... | collective-permute-start | bytes 786440 | tf_op jit(solution)/shard_map/ppermute | solution.py:24
  26.3 5.2 %collective-permute-start.1 = (bf16[2,512,128]{2,1,0:T(8,128)(2,1)S(1)}, bf16[2,512,128]{2,1,0:T(8,128)(2,1)S(1)}, u32[]{:S(2)}, u32[]{:S(2)}) collective-permute-start(bf16[2,512,128]{2,1,0:T(8,128)(2,1)S(1)} %shard_map.74), channel_id=1, source_target_pairs={{0,2},{2,4},{4,6},{6,8},{8,10},{10,12},{12,14},{14,16},{16,18},{18... | collective-permute-start | bytes 786440 | tf_op jit(solution)/shard_map/ppermute | solution.py:14
  31.6 1.3 %shard_map.82.refs_4_ = f32[2,512,128]{2,1,0:T(8,128)S(1)} custom-call(s32[3]{0:T(128)S(1)} %pad_add_fusion.1.where.refs_0_, bf16[2,1,512,1024]{3,2,1,0:T(8,128)(2,1)S(1)} %copy-done.2, bf16[2,512,128]{2,1,0:T(8,128)(2,1)S(1)} %collective-permute-done.13.refs_2_, bf16[2,512,128]{2,1,0:T(8,128)(2,1)S(1)} %collective-permute-done.14.refs_3_, ...), custom_call_target="tpu_custom_call" | custom-call | flops 268435456 | bytes 3670016 | tf_op jit(solution)/shard_map/pallas_call | solution.py:49
  32.9 1.3 %shard_map.83.refs_0_.refs_4_ = bf16[2,512,128]{2,1,0:T(8,128)(2,1)S(1)} custom-call(s32[3]{0:T(128)S(1)} %pad_add_fusion.1.where.refs_0_, bf16[2,1,512,1024]{3,2,1,0:T(8,128)(2,1)S(1)} %copy-done.3, bf16[2,512,128]{2,1,0:T(8,128)(2,1)S(1)} %collective-permute-done.11.refs_2_, bf16[2,512,128]{2,1,0:T(8,128)(2,1)S(1)} %collective-permute-done.12.refs_3_, ...), custom_call_target="tpu_custom_call" | custom-call | flops 268435456 | bytes 3407872 | tf_op jit(solution)/shard_map/pallas_call | solution.py:49
  34.1 1.9 %collective-permute-start.15 = (bf16[2,512,128]{2,1,0:T(8,128)(2,1)S(1)}, bf16[2,512,128]{2,1,0:T(8,128)(2,1)S(1)}, u32[]{:S(2)}, u32[]{:S(2)}) collective-permute-start(bf16[2,512,128]{2,1,0:T(8,128)(2,1)S(1)} %shard_map.83.refs_0_.refs_4_), channel_id=1, source_target_pairs={{0,1},{1,0},{2,3},{3,2},{4,5},{5,4},{6,7},{7,6},{8,9},{9,8},{10,11... | collective-permute-start | bytes 786440 | tf_op jit(solution)/shard_map/ppermute | solution.py:28
  36.1 1.9 %collective-permute-done.4.refs_3_ = bf16[2,512,128]{2,1,0:T(8,128)(2,1)S(1)} collective-permute-done((bf16[2,512,128]{2,1,0:T(8,128)(2,1)S(1)}, bf16[2,512,128]{2,1,0:T(8,128)(2,1)S(1)}, u32[]{:S(2)}, u32[]{:S(2)}) %collective-permute-start.4) | collective-permute-done | bytes 262176 | tf_op jit(solution)/shard_map/ppermute | solution.py:24
  39.2 2.5 %collective-permute-done.2.refs_3_ = bf16[2,512,128]{2,1,0:T(8,128)(2,1)S(1)} collective-permute-done((bf16[2,512,128]{2,1,0:T(8,128)(2,1)S(1)}, bf16[2,512,128]{2,1,0:T(8,128)(2,1)S(1)}, u32[]{:S(2)}, u32[]{:S(2)}) %collective-permute-start.2) | collective-permute-done | bytes 262176 | tf_op jit(solution)/shard_map/ppermute | solution.py:24
  42.9 2.2 %collective-permute-start.5 = (bf16[2,512,128]{2,1,0:T(8,128)(2,1)S(1)}, bf16[2,512,128]{2,1,0:T(8,128)(2,1)S(1)}, u32[]{:S(2)}, u32[]{:S(2)}) collective-permute-start(bf16[2,512,128]{2,1,0:T(8,128)(2,1)S(1)} %shard_map.76.refs_0_.refs_4_), channel_id=1, source_target_pairs={{0,1},{1,0},{2,3},{3,2},{4,5},{5,4},{6,7},{7,6},{8,9},{9,8},{10,11... | collective-permute-start | bytes 786440 | tf_op jit(solution)/shard_map/ppermute | solution.py:28
  47.2 3.4 %collective-permute-start.18 = (bf16[2,512,128]{2,1,0:T(8,128)(2,1)S(1)}, bf16[2,512,128]{2,1,0:T(8,128)(2,1)S(1)}, u32[]{:S(2)}, u32[]{:S(2)}) collective-permute-start(bf16[2,512,128]{2,1,0:T(8,128)(2,1)S(1)} %shard_map.85), channel_id=1, source_target_pairs={{0,4},{2,6},{4,8},{6,10},{8,12},{10,14},{12,16},{14,18},{16,20},{1... | collective-permute-start | bytes 786440 | tf_op jit(solution)/shard_map/ppermute | solution.py:14
  52.1 5.6 %collective-permute-done.5.refs_3_ = bf16[2,512,128]{2,1,0:T(8,128)(2,1)S(1)} collective-permute-done((bf16[2,512,128]{2,1,0:T(8,128)(2,1)S(1)}, bf16[2,512,128]{2,1,0:T(8,128)(2,1)S(1)}, u32[]{:S(2)}, u32[]{:S(2)}) %collective-permute-start.5) | collective-permute-done | bytes 262176 | tf_op jit(solution)/shard_map/ppermute | solution.py:28
  58.8 10.5 %collective-permute-start.9 = (bf16[2,512,128]{2,1,0:T(8,128)(2,1)S(1)}, bf16[2,512,128]{2,1,0:T(8,128)(2,1)S(1)}, u32[]{:S(2)}, u32[]{:S(2)}) collective-permute-start(bf16[2,512,128]{2,1,0:T(8,128)(2,1)S(1)} %shard_map.78), channel_id=1, source_target_pairs={{0,5},{1,4},{2,7},{3,6},{4,9},{5,8},{6,11},{7,10},{8,13},{9,12},{1... | collective-permute-start | bytes 786440 | tf_op jit(solution)/shard_map/ppermute | solution.py:24
  69.4 4.1 %collective-permute-done.8.refs_2_ = bf16[2,512,128]{2,1,0:T(8,128)(2,1)S(1)} collective-permute-done((bf16[2,512,128]{2,1,0:T(8,128)(2,1)S(1)}, bf16[2,512,128]{2,1,0:T(8,128)(2,1)S(1)}, u32[]{:S(2)}, u32[]{:S(2)}) %collective-permute-start.8) | collective-permute-done | bytes 262176 | tf_op jit(solution)/shard_map/ppermute | solution.py:14
  73.5 4.4 %collective-permute-start.7 = (bf16[2,512,128]{2,1,0:T(8,128)(2,1)S(1)}, bf16[2,512,128]{2,1,0:T(8,128)(2,1)S(1)}, u32[]{:S(2)}, u32[]{:S(2)}) collective-permute-start(bf16[2,512,128]{2,1,0:T(8,128)(2,1)S(1)} %shard_map.78), channel_id=1, source_target_pairs={{0,253},{1,252},{2,255},{3,254},{4,1},{5,0},{6,3},{7,2},{8,5},{9,4... | collective-permute-start | bytes 786440 | tf_op jit(solution)/shard_map/ppermute | solution.py:24
  80.5 1.4 %collective-permute-done.16.refs_2_ = bf16[2,512,128]{2,1,0:T(8,128)(2,1)S(1)} collective-permute-done((bf16[2,512,128]{2,1,0:T(8,128)(2,1)S(1)}, bf16[2,512,128]{2,1,0:T(8,128)(2,1)S(1)}, u32[]{:S(2)}, u32[]{:S(2)}) %collective-permute-start.16) | collective-permute-done | bytes 262176 | tf_op jit(solution)/shard_map/ppermute | solution.py:14
  81.8 7.9 %collective-permute-done.17.refs_3_ = bf16[2,512,128]{2,1,0:T(8,128)(2,1)S(1)} collective-permute-done((bf16[2,512,128]{2,1,0:T(8,128)(2,1)S(1)}, bf16[2,512,128]{2,1,0:T(8,128)(2,1)S(1)}, u32[]{:S(2)}, u32[]{:S(2)}) %collective-permute-start.17) | collective-permute-done | bytes 262176 | tf_op jit(solution)/shard_map/ppermute | solution.py:24
  89.8 2.1 %couple_last.2.refs_5_ = bf16[2,1,512,256]{3,2,1,0:T(8,128)(2,1)} custom-call(s32[3]{0:T(128)S(1)} %pad_add_fusion.where.refs_0_, bf16[2,1,512,1024]{3,2,1,0:T(8,128)(2,1)S(1)} %copy-done.5, bf16[2,512,128]{2,1,0:T(8,128)(2,1)S(1)} %collective-permute-done.16.refs_2_, bf16[2,512,128]{2,1,0:T(8,128)(2,1)S(1)} %collective-permute-done.17.refs_3_, ...), custom_call_target="tpu_custom_call" | custom-call | flops 268435456 | bytes 2097152 | tf_op jit(solution)/shard_map/couple_last/pallas_call | solution.py:209
  92.9 6.0 %collective-permute-done.7.refs_3_ = bf16[2,512,128]{2,1,0:T(8,128)(2,1)S(1)} collective-permute-done((bf16[2,512,128]{2,1,0:T(8,128)(2,1)S(1)}, bf16[2,512,128]{2,1,0:T(8,128)(2,1)S(1)}, u32[]{:S(2)}, u32[]{:S(2)}) %collective-permute-start.7) | collective-permute-done | bytes 262176 | tf_op jit(solution)/shard_map/ppermute | solution.py:24
  98.9 2.1 %couple_last.3 = bf16[2,1,512,256]{3,2,1,0:T(8,128)(2,1)} custom-call(s32[3]{0:T(128)S(1)} %pad_add_fusion.where.refs_0_, bf16[2,1,512,1024]{3,2,1,0:T(8,128)(2,1)S(1)} %copy-done.5, bf16[2,512,128]{2,1,0:T(8,128)(2,1)S(1)} %collective-permute-done.6.refs_2_, ...), custom_call_target="tpu_custom_call", output_to_operand_aliasing={{}: (5, {})} | custom-call | flops 268435456 | bytes 2097152 | tf_op jit(solution)/shard_map/couple_last/pallas_call | solution.py:209
  (50 shorter events, 18.6 us)
Async XLA Ops:
  1.0 8.8 %collective-permute-start.10 = (bf16[2,512,128]{2,1,0:T(8,128)(2,1)S(1)}, bf16[2,512,128]{2,1,0:T(8,128)(2,1)S(1)}, u32[]{:S(2)}, u32[]{:S(2)}) collective-permute-start(bf16[2,512,128]{2,1,0:T(8,128)(2,1)S(1)} %slice.8.refs_0_), channel_id=1, source_target_pairs={{0,1},{1,0},{2,3},{3,2},{4,5},{5,4},{6,7},{7,6},{8,9},{9,8},{10,11... | collective-permute-start | bytes 786440 | tf_op jit(solution)/shard_map/ppermute | solution.py:28
  3.9 17.8 %collective-permute-start = (bf16[2,512,128]{2,1,0:T(8,128)(2,1)S(1)}, bf16[2,512,128]{2,1,0:T(8,128)(2,1)S(1)}, u32[]{:S(2)}, u32[]{:S(2)}) collective-permute-start(bf16[2,512,128]{2,1,0:T(8,128)(2,1)S(1)} %slice.7.refs_0_), channel_id=1, source_target_pairs={{0,1},{1,0},{2,3},{3,2},{4,5},{5,4},{6,7},{7,6},{8,9},{9,8},{10,11... | collective-permute-start | bytes 786440 | tf_op jit(solution)/shard_map/ppermute | solution.py:28
  10.7 12.4 %collective-permute-start.13 = (bf16[2,512,128]{2,1,0:T(8,128)(2,1)S(1)}, bf16[2,512,128]{2,1,0:T(8,128)(2,1)S(1)}, u32[]{:S(2)}, u32[]{:S(2)}) collective-permute-start(bf16[2,512,128]{2,1,0:T(8,128)(2,1)S(1)} %shard_map.81), channel_id=1, source_target_pairs={{0,254},{2,0},{4,2},{6,4},{8,6},{10,8},{12,10},{14,12},{16,14},{18... | collective-permute-start | bytes 786440 | tf_op jit(solution)/shard_map/ppermute | solution.py:14
  13.5 12.9 %collective-permute-start.14 = (bf16[2,512,128]{2,1,0:T(8,128)(2,1)S(1)}, bf16[2,512,128]{2,1,0:T(8,128)(2,1)S(1)}, u32[]{:S(2)}, u32[]{:S(2)}) collective-permute-start(bf16[2,512,128]{2,1,0:T(8,128)(2,1)S(1)} %shard_map.81), channel_id=1, source_target_pairs={{0,255},{1,254},{2,1},{3,0},{4,3},{5,2},{6,5},{7,4},{8,7},{9,6},{1... | collective-permute-start | bytes 786440 | tf_op jit(solution)/shard_map/ppermute | solution.py:24
  15.3 16.3 %collective-permute-start.11 = (bf16[2,512,128]{2,1,0:T(8,128)(2,1)S(1)}, bf16[2,512,128]{2,1,0:T(8,128)(2,1)S(1)}, u32[]{:S(2)}, u32[]{:S(2)}) collective-permute-start(bf16[2,512,128]{2,1,0:T(8,128)(2,1)S(1)} %shard_map.81), channel_id=1, source_target_pairs={{0,2},{2,4},{4,6},{6,8},{8,10},{10,12},{12,14},{14,16},{16,18},{18... | collective-permute-start | bytes 786440 | tf_op jit(solution)/shard_map/ppermute | solution.py:14
  20.7 12.1 %collective-permute-start.12 = (bf16[2,512,128]{2,1,0:T(8,128)(2,1)S(1)}, bf16[2,512,128]{2,1,0:T(8,128)(2,1)S(1)}, u32[]{:S(2)}, u32[]{:S(2)}) collective-permute-start(bf16[2,512,128]{2,1,0:T(8,128)(2,1)S(1)} %shard_map.81), channel_id=1, source_target_pairs={{0,3},{1,2},{2,5},{3,4},{4,7},{5,6},{6,9},{7,8},{8,11},{9,10},{10,... | collective-permute-start | bytes 786440 | tf_op jit(solution)/shard_map/ppermute | solution.py:24
  21.7 9.9 %copy-start.2 = (bf16[2,1,512,1024]{3,2,1,0:T(8,128)(2,1)S(1)}, bf16[2,1,512,1024]{3,2,1,0:T(8,128)(2,1)}, u32[]{:S(2)}) copy-start(bf16[2,1,512,1024]{3,2,1,0:T(8,128)(2,1)} %refs_1_.18) | copy-start | bytes 6291460
  22.7 10.1 %copy-start.3 = (bf16[2,1,512,1024]{3,2,1,0:T(8,128)(2,1)S(1)}, bf16[2,1,512,1024]{3,2,1,0:T(8,128)(2,1)}, u32[]{:S(2)}) copy-start(bf16[2,1,512,1024]{3,2,1,0:T(8,128)(2,1)} %refs_1_.19) | copy-start | bytes 6291460
  22.7 13.3 %collective-permute-start.3 = (bf16[2,512,128]{2,1,0:T(8,128)(2,1)S(1)}, bf16[2,512,128]{2,1,0:T(8,128)(2,1)S(1)}, u32[]{:S(2)}, u32[]{:S(2)}) collective-permute-start(bf16[2,512,128]{2,1,0:T(8,128)(2,1)S(1)} %shard_map.74), channel_id=1, source_target_pairs={{0,254},{2,0},{4,2},{6,4},{8,6},{10,8},{12,10},{14,12},{16,14},{18... | collective-permute-start | bytes 786440 | tf_op jit(solution)/shard_map/ppermute | solution.py:14
  23.1 14.8 %collective-permute-start.4 = (bf16[2,512,128]{2,1,0:T(8,128)(2,1)S(1)}, bf16[2,512,128]{2,1,0:T(8,128)(2,1)S(1)}, u32[]{:S(2)}, u32[]{:S(2)}) collective-permute-start(bf16[2,512,128]{2,1,0:T(8,128)(2,1)S(1)} %shard_map.74), channel_id=1, source_target_pairs={{0,255},{1,254},{2,1},{3,0},{4,3},{5,2},{6,5},{7,4},{8,7},{9,6},{1... | collective-permute-start | bytes 786440 | tf_op jit(solution)/shard_map/ppermute | solution.py:24
  26.3 12.9 %collective-permute-start.1 = (bf16[2,512,128]{2,1,0:T(8,128)(2,1)S(1)}, bf16[2,512,128]{2,1,0:T(8,128)(2,1)S(1)}, u32[]{:S(2)}, u32[]{:S(2)}) collective-permute-start(bf16[2,512,128]{2,1,0:T(8,128)(2,1)S(1)} %shard_map.74), channel_id=1, source_target_pairs={{0,2},{2,4},{4,6},{6,8},{8,10},{10,12},{12,14},{14,16},{16,18},{18... | collective-permute-start | bytes 786440 | tf_op jit(solution)/shard_map/ppermute | solution.py:14
  31.5 10.1 %collective-permute-start.2 = (bf16[2,512,128]{2,1,0:T(8,128)(2,1)S(1)}, bf16[2,512,128]{2,1,0:T(8,128)(2,1)S(1)}, u32[]{:S(2)}, u32[]{:S(2)}) collective-permute-start(bf16[2,512,128]{2,1,0:T(8,128)(2,1)S(1)} %shard_map.74), channel_id=1, source_target_pairs={{0,3},{1,2},{2,5},{3,4},{4,7},{5,6},{6,9},{7,8},{8,11},{9,10},{10,... | collective-permute-start | bytes 786440 | tf_op jit(solution)/shard_map/ppermute | solution.py:24
  34.1 12.1 %collective-permute-start.15 = (bf16[2,512,128]{2,1,0:T(8,128)(2,1)S(1)}, bf16[2,512,128]{2,1,0:T(8,128)(2,1)S(1)}, u32[]{:S(2)}, u32[]{:S(2)}) collective-permute-start(bf16[2,512,128]{2,1,0:T(8,128)(2,1)S(1)} %shard_map.83.refs_0_.refs_4_), channel_id=1, source_target_pairs={{0,1},{1,0},{2,3},{3,2},{4,5},{5,4},{6,7},{7,6},{8,9},{9,8},{10,11... | collective-permute-start | bytes 786440 | tf_op jit(solution)/shard_map/ppermute | solution.py:28
  42.9 14.8 %collective-permute-start.5 = (bf16[2,512,128]{2,1,0:T(8,128)(2,1)S(1)}, bf16[2,512,128]{2,1,0:T(8,128)(2,1)S(1)}, u32[]{:S(2)}, u32[]{:S(2)}) collective-permute-start(bf16[2,512,128]{2,1,0:T(8,128)(2,1)S(1)} %shard_map.76.refs_0_.refs_4_), channel_id=1, source_target_pairs={{0,1},{1,0},{2,3},{3,2},{4,5},{5,4},{6,7},{7,6},{8,9},{9,8},{10,11... | collective-permute-start | bytes 786440 | tf_op jit(solution)/shard_map/ppermute | solution.py:28
  47.2 22.1 %collective-permute-start.18 = (bf16[2,512,128]{2,1,0:T(8,128)(2,1)S(1)}, bf16[2,512,128]{2,1,0:T(8,128)(2,1)S(1)}, u32[]{:S(2)}, u32[]{:S(2)}) collective-permute-start(bf16[2,512,128]{2,1,0:T(8,128)(2,1)S(1)} %shard_map.85), channel_id=1, source_target_pairs={{0,4},{2,6},{4,8},{6,10},{8,12},{10,14},{12,16},{14,18},{16,20},{1... | collective-permute-start | bytes 786440 | tf_op jit(solution)/shard_map/ppermute | solution.py:14
  51.5 26.4 %copy-start.4 = (bf16[2,1,512,1024]{3,2,1,0:T(8,128)(2,1)S(1)}, bf16[2,1,512,1024]{3,2,1,0:T(8,128)(2,1)}, u32[]{:S(2)}) copy-start(bf16[2,1,512,1024]{3,2,1,0:T(8,128)(2,1)} %refs_1_.21) | copy-start | bytes 6291460
  51.5 17.8 %collective-permute-start.19 = (bf16[2,512,128]{2,1,0:T(8,128)(2,1)S(1)}, bf16[2,512,128]{2,1,0:T(8,128)(2,1)S(1)}, u32[]{:S(2)}, u32[]{:S(2)}) collective-permute-start(bf16[2,512,128]{2,1,0:T(8,128)(2,1)S(1)} %shard_map.85), channel_id=1, source_target_pairs={{0,5},{1,4},{2,7},{3,6},{4,9},{5,8},{6,11},{7,10},{8,13},{9,12},{1... | collective-permute-start | bytes 786440 | tf_op jit(solution)/shard_map/ppermute | solution.py:24
  58.7 14.8 %collective-permute-start.8 = (bf16[2,512,128]{2,1,0:T(8,128)(2,1)S(1)}, bf16[2,512,128]{2,1,0:T(8,128)(2,1)S(1)}, u32[]{:S(2)}, u32[]{:S(2)}) collective-permute-start(bf16[2,512,128]{2,1,0:T(8,128)(2,1)S(1)} %shard_map.78), channel_id=1, source_target_pairs={{0,4},{2,6},{4,8},{6,10},{8,12},{10,14},{12,16},{14,18},{16,20},{1... | collective-permute-start | bytes 786440 | tf_op jit(solution)/shard_map/ppermute | solution.py:14
  58.8 20.4 %collective-permute-start.9 = (bf16[2,512,128]{2,1,0:T(8,128)(2,1)S(1)}, bf16[2,512,128]{2,1,0:T(8,128)(2,1)S(1)}, u32[]{:S(2)}, u32[]{:S(2)}) collective-permute-start(bf16[2,512,128]{2,1,0:T(8,128)(2,1)S(1)} %shard_map.78), channel_id=1, source_target_pairs={{0,5},{1,4},{2,7},{3,6},{4,9},{5,8},{6,11},{7,10},{8,13},{9,12},{1... | collective-permute-start | bytes 786440 | tf_op jit(solution)/shard_map/ppermute | solution.py:24
  69.3 12.5 %collective-permute-start.16 = (bf16[2,512,128]{2,1,0:T(8,128)(2,1)S(1)}, bf16[2,512,128]{2,1,0:T(8,128)(2,1)S(1)}, u32[]{:S(2)}, u32[]{:S(2)}) collective-permute-start(bf16[2,512,128]{2,1,0:T(8,128)(2,1)S(1)} %shard_map.85), channel_id=1, source_target_pairs={{0,252},{2,254},{4,0},{6,2},{8,4},{10,6},{12,8},{14,10},{16,12},{1... | collective-permute-start | bytes 786440 | tf_op jit(solution)/shard_map/ppermute | solution.py:14
  69.3 20.5 %collective-permute-start.17 = (bf16[2,512,128]{2,1,0:T(8,128)(2,1)S(1)}, bf16[2,512,128]{2,1,0:T(8,128)(2,1)S(1)}, u32[]{:S(2)}, u32[]{:S(2)}) collective-permute-start(bf16[2,512,128]{2,1,0:T(8,128)(2,1)S(1)} %shard_map.85), channel_id=1, source_target_pairs={{0,253},{1,252},{2,255},{3,254},{4,1},{5,0},{6,3},{7,2},{8,5},{9,4... | collective-permute-start | bytes 786440 | tf_op jit(solution)/shard_map/ppermute | solution.py:24
  69.3 23.6 %collective-permute-start.6 = (bf16[2,512,128]{2,1,0:T(8,128)(2,1)S(1)}, bf16[2,512,128]{2,1,0:T(8,128)(2,1)S(1)}, u32[]{:S(2)}, u32[]{:S(2)}) collective-permute-start(bf16[2,512,128]{2,1,0:T(8,128)(2,1)S(1)} %shard_map.78), channel_id=1, source_target_pairs={{0,252},{2,254},{4,0},{6,2},{8,4},{10,6},{12,8},{14,10},{16,12},{1... | collective-permute-start | bytes 786440 | tf_op jit(solution)/shard_map/ppermute | solution.py:14
  73.5 25.4 %collective-permute-start.7 = (bf16[2,512,128]{2,1,0:T(8,128)(2,1)S(1)}, bf16[2,512,128]{2,1,0:T(8,128)(2,1)S(1)}, u32[]{:S(2)}, u32[]{:S(2)}) collective-permute-start(bf16[2,512,128]{2,1,0:T(8,128)(2,1)S(1)} %shard_map.78), channel_id=1, source_target_pairs={{0,253},{1,252},{2,255},{3,254},{4,1},{5,0},{6,3},{7,2},{8,5},{9,4... | collective-permute-start | bytes 786440 | tf_op jit(solution)/shard_map/ppermute | solution.py:24
  79.2 10.6 %copy-start.5 = (bf16[2,1,512,1024]{3,2,1,0:T(8,128)(2,1)S(1)}, bf16[2,1,512,1024]{3,2,1,0:T(8,128)(2,1)}, u32[]{:S(2)}) copy-start(bf16[2,1,512,1024]{3,2,1,0:T(8,128)(2,1)} %refs_1_.23) | copy-start | bytes 6291460
  (3 other events, 17.5 us)
